TPU v7x, 32 devices: a whole 2x2x4 slice. The times are simulated.
32 devices in a mesh: dp: 16 (over z, y, x), ctx: 2 (over core).
Axes of the slice: x: 2, y: 2, z: 4, core: 2. Of those that a mesh axis runs over, the one named last changes fastest.
Arguments:
- layer_in: bfloat16 [16, 256, 4096], P('dp', 'ctx'), may hold values from -6 to 6
- inner_act: bfloat16 [16, 256, 2176], P('dp', 'ctx'), may hold values from -6 to 6
- readout: bfloat16 [16, 256, 64], P('dp', 'ctx'), may hold values from -0.75 to 0.75
- w_in: bfloat16 [4096, 132], P('dp'), may hold values from -0.09375 to 0.09375
- a_log: float32 [68], replicated, may hold values from -3.9 to -1.6
- dt_bias: float32 [68], replicated, may hold values from -4 to -1
- d_skip: float32 [68], replicated, may hold values from 0.5 to 1.5
- grad_out: bfloat16 [16, 256, 2176], P('dp', 'ctx'), may hold values from -6 to 6
Outputs:
- grad_x: bfloat16 [16, 256, 2176], P('dp', 'ctx')
- grad_c: bfloat16 [16, 256, 64], P('dp', 'ctx')
- grad_proj: bfloat16 [16, 256, 132], P('dp', 'ctx')
- grad_w: float32 [4096, 132], P('dp', 'ctx')
All inputs are finite; a program needn't handle non-finite values.
Results may differ from a plain program's by a relative error of at most 0.015.
Values may be sent and summed in bfloat16 or wider, within the bound.
A program may use at most 64 MiB of HBM per device.

v0:
```python
import jax
import jax.numpy as jnp
from jax import lax
from jax.sharding import PartitionSpec as P

STATE = 64
BLOCK = 128


def entering(array, axis, join, neutral, backward):
    count = lax.axis_size(axis)
    place = lax.axis_index(axis)
    ahead = count - 1 - place if backward else place
    gathered = jax.tree.map(
        lambda a, kind: lax.all_gather(a.astype(kind), axis), array, (jnp.bfloat16, jnp.bfloat16)
    )
    state = jax.tree.map(lambda a, e: jnp.zeros_like(a) + jnp.asarray(e, a.dtype), array, neutral)

    def one(turn, state):
        source = count - 1 - turn if backward else turn
        return join(
            state,
            jax.tree.map(
                lambda a, own: lax.dynamic_index_in_dim(a, source, 0, False).astype(own.dtype),
                gathered,
                array,
            ),
        )

    return lax.fori_loop(0, ahead, one, state)


def prepare(projected, a_log, dt_bias):
    b_rows = projected[:, :STATE].astype(jnp.bfloat16)
    step_size = jax.nn.softplus(projected[:, STATE:] + dt_bias)
    decay_rate = -jnp.exp(a_log) * step_size
    return (b_rows, step_size, decay_rate)


def blocked(values, width):
    return values.reshape(values.shape[0] // BLOCK, BLOCK, width)


def split_blocks(projected, inner_rows, a_log, dt_bias):
    row_count = projected.shape[0]
    head_count = a_log.shape[0]
    head_width = inner_rows.shape[1] // head_count
    b_rows, step_size, decay_rate = prepare(projected, a_log, dt_bias)
    inner_blocks = inner_rows.reshape(row_count // BLOCK, BLOCK, head_count, head_width)
    step_blocks = jnp.swapaxes(blocked(step_size, head_count), 1, 2)
    cum_blocks = jnp.cumsum(jnp.swapaxes(blocked(decay_rate, head_count), 1, 2), axis=2)
    return (inner_blocks, blocked(b_rows, STATE), step_blocks, cum_blocks, decay_rate)


def state_input(inner_c, b_c, step_c, cum_c):
    to_end = jnp.exp(cum_c[:, -1:] - cum_c) * step_c
    weighted = (b_c.astype(jnp.float32)[None] * to_end[:, :, None]).astype(jnp.bfloat16)
    return jnp.einsum("shp,hsn->hpn", inner_c, weighted, preferred_element_type=jnp.float32)


def block_forward(projected, inner_rows, c_rows, a_log, dt_bias, d_skip, entry_state):
    row_count = projected.shape[0]
    inner_blocks, b_blocks, step_blocks, cum_blocks, decay_rate = split_blocks(
        projected, inner_rows, a_log, dt_bias
    )
    c_blocks = blocked(c_rows, STATE)
    position = jnp.arange(BLOCK)
    causal = position[:, None] >= position[None, :]

    def block_advance(carried, pieces):
        inner_c, b_c, c_c, step_c, cum_c = pieces
        scores = jnp.dot(c_c, b_c.T, preferred_element_type=jnp.float32)
        spread = cum_c[:, :, None] - cum_c[:, None, :]
        factor = jnp.where(causal, jnp.exp(jnp.where(causal, spread, 0.0)), 0.0)
        mixing = (scores[None] * factor * step_c[:, None, :]).astype(jnp.bfloat16)
        within = jnp.einsum("hts,shp->thp", mixing, inner_c, preferred_element_type=jnp.float32)
        added = state_input(inner_c, b_c, step_c, cum_c)
        carried_in = jnp.einsum(
            "tn,hpn->thp", c_c.astype(jnp.float32), carried, precision=lax.Precision.HIGHEST
        )
        carried_in = carried_in * jnp.exp(cum_c).T[:, :, None]
        result = (within + carried_in + d_skip[None, :, None] * inner_c.astype(jnp.float32)).astype(
            jnp.bfloat16
        )
        carried = jnp.exp(cum_c[:, -1])[:, None, None] * carried + added
        return (carried, result)

    final_state, outputs = lax.scan(
        block_advance, entry_state, (inner_blocks, b_blocks, c_blocks, step_blocks, cum_blocks)
    )
    return (outputs.reshape(row_count, inner_rows.shape[1]), final_state)


def local_summary(projected, inner_rows, a_log, dt_bias):
    inner_blocks, b_blocks, step_blocks, cum_blocks, decay_rate = split_blocks(
        projected, inner_rows, a_log, dt_bias
    )
    head_count = a_log.shape[0]
    head_width = inner_rows.shape[1] // head_count

    def local_advance(carried, pieces):
        inner_c, b_c, step_c, cum_c = pieces
        added = state_input(inner_c, b_c, step_c, cum_c)
        return (jnp.exp(cum_c[:, -1])[:, None, None] * carried + added, None)

    zero_state = jnp.zeros((head_count, head_width, STATE), jnp.float32)
    final_state, unused = lax.scan(
        local_advance, zero_state, (inner_blocks, b_blocks, step_blocks, cum_blocks)
    )
    return (jnp.exp(jnp.sum(decay_rate, axis=0)), final_state)


def entry_weights(projected, c_rows, grad_rows, a_log, dt_bias):
    b_rows, step_size, decay_rate = prepare(projected, a_log, dt_bias)
    row_count = projected.shape[0]
    head_count = a_log.shape[0]
    head_width = grad_rows.shape[1] // head_count
    growth = jnp.exp(jnp.cumsum(decay_rate, axis=0))
    weighted = (c_rows.astype(jnp.float32)[:, None, :] * growth[:, :, None]).astype(jnp.bfloat16)
    return jnp.einsum(
        "thp,thn->hpn",
        grad_rows.reshape(row_count, head_count, head_width),
        weighted,
        preferred_element_type=jnp.float32,
    )


def combine_carry(earlier, later):
    return (earlier[0] * later[0], later[1] + later[0][:, None, None] * earlier[1])


def pass_along(decay_total, summary, backward):
    identity = (jnp.ones_like(decay_total), jnp.zeros_like(summary))
    return entering((decay_total, summary), "ctx", combine_carry, identity, backward)


def per_device(layer_in, inner_act, readout, w_in, a_log, dt_bias, d_skip, grad_out):
    tokens = layer_in[0]
    inner_rows = inner_act[0]
    c_rows = readout[0]
    grad_rows = grad_out[0]
    w_full = lax.all_gather(w_in, "dp", axis=0, tiled=True)
    projected = jnp.dot(tokens, w_full, preferred_element_type=jnp.float32)
    decay_total, own_state = local_summary(projected, inner_rows, a_log, dt_bias)
    entry_part = entry_weights(projected, c_rows, grad_rows, a_log, dt_bias)
    entry_state = pass_along(decay_total, own_state, False)[1]
    exit_grad = pass_along(decay_total, entry_part, True)[1]

    def recompute(proj_val, inner_val, c_val):
        return block_forward(proj_val, inner_val, c_val, a_log, dt_bias, d_skip, entry_state)

    primal, pullback = jax.vjp(recompute, projected, inner_rows, c_rows)
    grad_p, grad_v, grad_r = pullback((grad_rows, exit_grad))
    proj_grad = grad_p.astype(jnp.bfloat16)
    seq_count = lax.axis_size("dp")
    contract = (((0,), (0,)), ((), ()))
    summed = lax.psum_scatter(
        lax.dot_general(tokens, proj_grad, contract, preferred_element_type=jnp.float32),
        "dp",
        scatter_dimension=0,
        tiled=True,
    )
    weight_grad = lax.psum_scatter(summed, "ctx", scatter_dimension=1, tiled=True)
    return (grad_v[None], grad_r[None], proj_grad[None], weight_grad / seq_count)


def solution(mesh):
    in_specs = (
        P("dp", "ctx", None),
        P("dp", "ctx", None),
        P("dp", "ctx", None),
        P("dp", None),
        P(),
        P(),
        P(),
        P("dp", "ctx", None),
    )
    out_specs = (P("dp", "ctx", None), P("dp", "ctx", None), P("dp", "ctx", None), P("dp", "ctx"))
    return jax.shard_map(
        per_device, mesh=mesh, in_specs=in_specs, out_specs=out_specs, check_vma=False
    )
```

profile of v0, /device:TPU:0, one launch (start us, length us, event | category | flops | bytes accessed | tf_op | source)
XLA Modules:
  0.0 213.8 jit_solution(7782846302152594224)
XLA Ops:
  8.0 1.4 copy.64
  9.4 1.1 copy.76
  12.5 56.9 %all-gather.5.cloned.1.call-done = bf16[4096,132]{0,1:T(8,128)(2,1)} async-done(((bf16[256,132]{0,1:T(8,128)(2,1)}), bf16[4096,132]{0,1:T(8,128)(2,1)}) %all-gather.5.cloned.1.call-update) | async-done | bytes 1081360 | tf_op jit(solution)/shard_map/all_gather | solution.py:142
  69.4 1.7 fusion.46
  74.6 2.6 %all-gather = bf16[136,32,64]{2,1,0:T(8,128)(2,1)S(1)} all-gather(bf16[68,32,64]{2,1,0:T(8,128)(2,1)S(1)} %fusion.29), channel_id=2, replica_groups=mesh['dp'=16,'ctx'=2] {'ctx'}, dimensions={0}, use_global_device_ids=true | all-gather | bytes 835584 | tf_op jit(solution)/shard_map/all_gather | solution.py:15
  77.5 2.4 %all-reduce.4 = bf16[136]{0:T(256)(128)(2,1)S(1)} all-reduce(bf16[136]{0:T(256)(128)(2,1)S(1)} %dynamic-update-slice), channel_id=3, replica_groups=mesh['dp'=16,'ctx'=2] {'ctx'}, use_global_device_ids=true, to_apply=%add.4 | all-reduce | flops 136 | bytes 544
  80.5 2.4 %fusion.13 = (f32[68,128]{1,0:T(8,128)}, bf16[128,64]{0,1:T(8,128)(2,1)}) fusion(f32[128,64]{0,1:T(8,128)} %fusion.68, f32[68,128]{1,0:T(8,128)} %copy.69, f32[68,32,64]{2,1,0:T(8,128)S(1)} %get-tuple-element.513, bf16[128,68,32]{0,2,1:T(8,128)(2,1)} %bitcast.174), kind=kOutput, calls=%fused_computation.23 | convolution fusion | flops 38419968 | bytes 1232896 | tf_op jit(solution)/shard_map/transpose(jvp())/while/body/eval_jaxpr/shp,hsn->hpn/dot_general | solution.py:58
  83.6 2.7 %all-gather.2 = bf16[136,32,64]{2,1,0:T(8,128)(2,1)} all-gather(bf16[68,32,64]{2,1,0:T(8,128)(2,1)S(1)} %fusion.28), channel_id=4, replica_groups=mesh['dp'=16,'ctx'=2] {'ctx'}, dimensions={0}, use_global_device_ids=true | all-gather | bytes 835584 | tf_op jit(solution)/shard_map/all_gather | solution.py:15
  87.7 1.3 fusion.27
  89.9 0.9 copy.78
  92.7 1.5 copy.80
  94.2 1.6 copy.70
  95.7 6.0 %fusion.11 = (f32[68,128]{1,0:T(8,128)}, f32[68,128]{1,0:T(8,128)}, f32[68,128]{1,0:T(8,128)}, bf16[128,128]{1,0:T(8,128)(2,1)}) fusion(f32[68,128]{1,0:T(8,128)} %copy.73, f32[68,128]{1,0:T(8,128)} %bitcast.177, f32[128,128]{1,0:T(8,128)} %copy.70, pred[128,128]{1,0:T(8,128)(4,1)} %iota_compare_fusion, bf16[68,32,128]{2,1,0:T(8,128)(2,1)} %bitcast.164, ...), kind=kOutput, calls=%fused_computation.19 | convolution fusion | flops 90200576 | bytes 1402880 | tf_op jit(solution)/shard_map/transpose(jvp())/while/body/eval_jaxpr/hts,shp->thp/dot_general | solution.py:76
  101.7 1.5 copy.82
  103.2 1.5 copy.83
  104.7 1.6 fusion.57
  106.2 0.9 copy.84
  107.2 1.9 reduce_window_sum.37
  109.0 1.5 copy.85
  110.5 1.5 copy.79
  112.0 1.4 copy.86
  113.4 1.0 fusion.50
  114.4 1.0 fusion.41
  115.4 1.9 convolution_bitcast_fusion
  118.2 1.1 bitcast_multiply_fusion.2
  119.4 2.0 fusion.42
  121.4 1.5 fusion.44
  123.0 2.0 fusion.30
  125.5 72.9 %reduce-scatter.4.cloned.1.call-done = f32[256,132]{0,1:T(8,128)} async-done(((f32[4096,132]{0,1:T(8,128)}), f32[256,132]{0,1:T(8,128)}) %reduce-scatter.4.cloned.1.call-update) | async-done | bytes 135184 | tf_op jit(solution)/shard_map/reduce_scatter | solution.py:157
  198.4 3.6 %fusion = f32[256,72]{0,1:T(8,128)S(1)} fusion(f32[256,132]{0,1:T(8,128)} %reduce-scatter.4.cloned.1.call-done), kind=kCustom, calls=%all-reduce-scatter | all-reduce-scatter fusion | flops 36865 | bytes 209408
  202.0 2.3 %collective-permute-start = (f32[256,6]{0,1:T(8,128)S(1)}, f32[256,6]{0,1:T(8,128)S(1)}, u32[]{:S(2)}, u32[]{:S(2)}) collective-permute-start(f32[256,6]{0,1:T(8,128)S(1)} %slice.28), channel_id=1, source_target_pairs={{0,1},{2,3},{4,5},{6,7},{8,9},{10,11},{12,13},{14,15},{16,17},{18,... | collective-permute-start | bytes 18440
  205.1 1.1 copy.88
  (101 shorter events, 13.7 us)
Async XLA Ops:
  7.2 62.2 %copy-start = (bf16[1,128,4096]{2,1,0:T(8,128)(2,1)S(1)}, bf16[1,128,4096]{2,1,0:T(8,128)(2,1)}, u32[]{:S(2)}) copy-start(bf16[1,128,4096]{2,1,0:T(8,128)(2,1)} %param.12) | copy-start | bytes 3145732
  7.2 2.2 %copy-start.4 = (bf16[1,128,2176]{2,1,0:T(8,128)(2,1)S(1)}, bf16[1,128,2176]{2,1,0:T(8,128)(2,1)}, u32[]{:S(2)}) copy-start(bf16[1,128,2176]{2,1,0:T(8,128)(2,1)} %param.13) | copy-start | bytes 1671172
  7.2 62.2 %all-gather.5.cloned.1.call-start = ((), (), s32[]{:S(2)}) async-start(), calls=%async_computation.1 | async-start | bytes 1183744 | tf_op jit(solution)/shard_map/all_gather | solution.py:142
  7.9 190.4 %reduce-scatter.4.cloned.1.call-start = ((), (), s32[]{:S(2)}) async-start(), calls=%async_computation.2 | async-start | bytes 2367488 | tf_op jit(solution)/shard_map/reduce_scatter | solution.py:157
  8.0 2.5 %copy-start.24 = (u32[32]{0:T(128)S(1)}, u32[32]{0:T(128)}, u32[]{:S(2)}) copy-start(u32[32]{0:T(128)} %constant.223) | copy-start | bytes 388
  8.0 4.4 %copy-start.26 = (f32[68]{0:T(128)S(1)}, f32[68]{0:T(128)}, u32[]{:S(2)}) copy-start(f32[68]{0:T(128)} %param.16) | copy-start | bytes 820
  8.0 4.4 %copy-start.7 = (bf16[1,128,64]{1,2,0:T(8,128)(2,1)S(1)}, bf16[1,128,64]{1,2,0:T(8,128)(2,1)}, u32[]{:S(2)}) copy-start(bf16[1,128,64]{1,2,0:T(8,128)(2,1)} %param.14) | copy-start | bytes 49156
  9.4 64.6 %copy-start.1 = (bf16[1,128,2176]{1,2,0:T(8,128)(2,1)}, bf16[1,128,2176]{1,2,0:T(8,128)(2,1)S(1)}, u32[]{:S(2)}) copy-start(bf16[1,128,2176]{1,2,0:T(8,128)(2,1)S(1)} %copy.64) | copy-start | bytes 1671172
  12.4 59.4 %copy-start.23 = (f32[68]{0:T(128)}, f32[68]{0:T(128)S(1)}, u32[]{:S(2)}) copy-start(f32[68]{0:T(128)S(1)} %exponential_negate_fusion) | copy-start | bytes 820
  12.4 59.4 %copy-start.22 = (f32[68]{0:T(128)S(1)}, f32[68]{0:T(128)}, u32[]{:S(2)}) copy-start(f32[68]{0:T(128)} %param.17) | copy-start | bytes 820
  71.1 18.0 %copy-start.6 = (f32[128,132]{0,1:T(8,128)}, f32[128,132]{0,1:T(8,128)S(1)}, u32[]{:S(2)}) copy-start(f32[128,132]{0,1:T(8,128)S(1)} %fusion.46) | copy-start | bytes 202756
  72.3 0.6 copy-start.11
  72.9 18.6 %copy-start.21 = (f32[68]{0:T(128)}, f32[68]{0:T(128)S(1)}, u32[]{:S(2)}) copy-start(f32[68]{0:T(128)S(1)} %slice_bitcast_fusion) | copy-start | bytes 820
  80.5 2.4 %copy-start.5 = (bf16[1,128,2176]{1,2,0:T(8,128)(2,1)S(1)}, bf16[1,128,2176]{1,2,0:T(8,128)(2,1)}, u32[]{:S(2)}) copy-start(bf16[1,128,2176]{1,2,0:T(8,128)(2,1)} %copy.76) | copy-start | bytes 1671172
  80.5 2.4 %copy-start.13 = (f32[68,128]{1,0:T(8,128)S(1)}, f32[68,128]{1,0:T(8,128)}, u32[]{:S(2)}) copy-start(f32[68,128]{1,0:T(8,128)} %copy.69) | copy-start | bytes 104452
  80.5 2.4 %copy-start.15 = (f32[128,64]{0,1:T(8,128)S(1)}, f32[128,64]{0,1:T(8,128)}, u32[]{:S(2)}) copy-start(f32[128,64]{0,1:T(8,128)} %fusion.68) | copy-start | bytes 98308
  86.7 1.1 copy-start.2
  86.7 1.0 copy-start.8
  101.7 12.7 %copy-start.9 = (bf16[1,128,64]{1,2,0:T(8,128)(2,1)S(1)}, bf16[1,128,64]{1,2,0:T(8,128)(2,1)}, u32[]{:S(2)}) copy-start(bf16[1,128,64]{1,2,0:T(8,128)(2,1)} %param.14) | copy-start | bytes 49156
  117.3 0.8 copy-start.10
  119.4 2.0 copy-start.17
  119.4 3.6 %copy-start.3 = (bf16[1,128,2176]{1,2,0:T(8,128)(2,1)S(1)}, bf16[1,128,2176]{1,2,0:T(8,128)(2,1)}, u32[]{:S(2)}) copy-start(bf16[1,128,2176]{1,2,0:T(8,128)(2,1)} %copy-done.1) | copy-start | bytes 1671172
  119.4 3.5 %copy-start.12 = (f32[1,68,128]{2,1,0:T(8,128)S(1)}, f32[1,68,128]{2,1,0:T(8,128)}, u32[]{:S(2)}) copy-start(f32[1,68,128]{2,1,0:T(8,128)} %copy-done.11) | copy-start | bytes 104452
  119.4 3.5 %copy-start.18 = (f32[128,128]{1,0:T(8,128)S(1)}, f32[128,128]{1,0:T(8,128)}, u32[]{:S(2)}) copy-start(f32[128,128]{1,0:T(8,128)} %copy.70) | copy-start | bytes 196612
  119.4 3.5 %copy-start.19 = (f32[68,128]{1,0:T(8,128)S(1)}, f32[68,128]{1,0:T(8,128)}, u32[]{:S(2)}) copy-start(f32[68,128]{1,0:T(8,128)} %copy.73) | copy-start | bytes 104452
  119.4 3.5 %copy-start.20 = (pred[128,128]{1,0:T(8,128)(4,1)S(1)}, pred[128,128]{1,0:T(8,128)(4,1)}, u32[]{:S(2)}) copy-start(pred[128,128]{1,0:T(8,128)(4,1)} %iota_compare_fusion) | copy-start | bytes 49156
  123.0 2.0 copy-start.14
  123.0 2.0 copy-start.16
  123.0 2.0 copy-start.25
  202.0 4.1 %collective-permute-start = (f32[256,6]{0,1:T(8,128)S(1)}, f32[256,6]{0,1:T(8,128)S(1)}, u32[]{:S(2)}, u32[]{:S(2)}) collective-permute-start(f32[256,6]{0,1:T(8,128)S(1)} %slice.28), channel_id=1, source_target_pairs={{0,1},{2,3},{4,5},{6,7},{8,9},{10,11},{12,13},{14,15},{16,17},{18,... | collective-permute-start | bytes 18440
Sparse Core Ops, SparseCore 0:
  10.7 58.5 all-gather.4
  117.5 80.8 reduce-scatter.3
where the time goes:
time: 215 us; the launch traced here: 214 us
  waiting for transfers between devices  130 us (60%)
  matrix products  22.4 us (10%)
  local copies, waits for them, and re-layouts  20.8 us (10%)
  between operations  15.9 us (7%)
  blocking collectives  11.4 us (5%)
  other arithmetic  10.2 us (5%)
  starting transfers between devices  2.33 us (1%)
    reduce_scatter x1, waiting for transfers between devices, per_device(): lax.psum_scatter(lax.dot_general(tokens, proj_grad, contract, preferred_e...  72.9 us
    all_gather x1, waiting for transfers between devices, per_device(): w_full = lax.all_gather(w_in, 'dp', axis=0, tiled=True)  56.9 us
    dot_general x2, matrix products, block_advance(): jnp.einsum('hts,shp->thp', mixing, inner_c, preferred_element_type=jnp.fl...  7.92 us
    unnamed x64, local copies, waits for them, and re-layouts  6.5 us
    unnamed x2, blocking collectives  6.08 us
    all_gather x2, blocking collectives, entering(): lax.all_gather(a.astype(kind), axis)  5.35 us
  transfers between devices with their start and end apart: 3, of which 2 were waited for; matrix products, arithmetic and copies ran while one was open for 6% of the time, Pallas kernels for 0%

commit v1 on v0

v1 whole, which is shorter than its diff:
```python
import functools

import jax
import jax.numpy as jnp
from jax import lax
from jax.experimental import pallas as pl
from jax.experimental.pallas import tpu as pltpu
from jax.sharding import PartitionSpec as P

STATE = 64
LANES = 128
MESH = pl.DeviceIdType.MESH
F32 = jnp.float32
BF16 = jnp.bfloat16


def up(n, m):
    return -(-n // m) * m


def dot(a, b):
    return jnp.dot(a, b, preferred_element_type=F32)


def dot_nt(a, b):
    return lax.dot_general(a, b, (((1,), (1,)), ((), ())), preferred_element_type=F32)


def split(v):
    hi = v.astype(BF16)
    return hi, (v - hi.astype(F32)).astype(BF16)


def dot_split(v, b):
    hi, lo = split(v)
    return dot(hi, b) + dot(lo, b)


def dot_exact(sel, v):
    hi, rest = v.astype(BF16), None
    rest = v - hi.astype(F32)
    mid, low = split(rest)
    return dot(sel, hi) + dot(sel, mid) + dot(sel, low)


def iota(shape, dim):
    return lax.broadcasted_iota(jnp.int32, shape, dim)


def kernel(cfg, tok, x, g, c, w, vec, dexp, gx, gc, gp, gw, wall, trecv, gall, sloc, crecv, sin, gin,
           xw, gwt, dx, proj, cum_r, dt_r, cumt, rowt, qacc, ds, sv, sg, db2, dc2, gpt, part, pst, precv,
           decs, decr, gs, ws, wr, as_, ar, gsn, gr, cs, cr, ps, pr, es, er):
    n_dp, n_ctx, t, rows, heads, width, cols = cfg
    wide = rows % LANES == 0
    groups = x.shape[1] // LANES
    gh = LANES // width
    cb = cols // n_ctx
    cbp = up(cb, 8)
    me = lax.axis_index("dp")
    my = lax.axis_index("ctx")

    def peer(k):
        return lax.rem(me + k, n_dp)

    def mate(k):
        return lax.rem(my + k, n_ctx)

    def col(ref, i):
        return ref.at[:, pl.ds(pl.multiple_of(i * rows, LANES), rows)] if wide else ref.at[i]

    def blk(i):
        return pl.ds(pl.multiple_of(i * t, LANES), t)

    def lanes(q):
        return pl.ds(pl.multiple_of(q * LANES, LANES), LANES)

    barrier = pltpu.get_barrier_semaphore()

    def greet(k, carry):
        pl.semaphore_signal(barrier, inc=1, device_id=(peer(k), my), device_id_type=MESH)
        return carry

    def greet_mate(k, carry):
        pl.semaphore_signal(barrier, inc=1, device_id=(me, mate(k)), device_id_type=MESH)
        return carry

    lax.fori_loop(1, n_dp, greet, 0)
    lax.fori_loop(1, n_ctx, greet_mate, 0)
    pl.semaphore_wait(barrier, n_dp + n_ctx - 2)

    def w_copy(k):
        return pltpu.make_async_remote_copy(
            src_ref=w, dst_ref=col(wall, me), send_sem=ws.at[k], recv_sem=wr.at[k],
            device_id=(peer(k), my), device_id_type=MESH)

    def a_copy(k):
        return pltpu.make_async_remote_copy(
            src_ref=col(tok, peer(k)), dst_ref=trecv.at[blk(me), :], send_sem=as_.at[k],
            recv_sem=ar.at[k], device_id=(peer(k), my), device_id_type=MESH)

    def g_copy(k):
        return pltpu.make_async_remote_copy(
            src_ref=gpt, dst_ref=gall.at[:, blk(me)], send_sem=gsn.at[k], recv_sem=gr.at[k],
            device_id=(peer(k), my), device_id_type=MESH)

    def c_copy(k):
        other = mate(k)
        which = jnp.where(other > my, 0, 1)
        return pltpu.make_async_remote_copy(
            src_ref=sloc.at[which], dst_ref=crecv.at[my], send_sem=cs.at[k], recv_sem=cr.at[k],
            device_id=(me, other), device_id_type=MESH)

    def d_copy(k):
        return pltpu.make_async_remote_copy(
            src_ref=decs, dst_ref=decr.at[my], send_sem=es.at[k], recv_sem=er.at[k],
            device_id=(me, mate(k)), device_id_type=MESH)

    def p_copy(k):
        return pltpu.make_async_remote_copy(
            src_ref=pst.at[mate(k)], dst_ref=precv.at[my], send_sem=ps.at[k], recv_sem=pr.at[k],
            device_id=(me, mate(k)), device_id_type=MESH)

    def each(n, act):
        def step(k, carry):
            act(k)
            return carry

        lax.fori_loop(1, n, step, 0)

    each(n_dp, lambda k: w_copy(k).start())
    if wide:
        wall[:, pl.ds(pl.multiple_of(me * rows, LANES), rows)] = w[...]
        trecv[blk(me), :] = tok[:, pl.ds(pl.multiple_of(me * rows, LANES), rows)]
    else:
        wall[me] = w[...]
        trecv[blk(me), :] = tok[me]
    proj[...] = jnp.zeros_like(proj)
    qacc[...] = jnp.zeros_like(qacc)
    ds[...] = jnp.zeros_like(ds)
    for ref in (sv, sg, db2, dc2):
        ref[...] = jnp.zeros_like(ref)
    each(n_dp, lambda k: w_copy(k).wait_recv())
    each(n_dp, lambda k: a_copy(k).start())
    wcols = w.shape[0]
    if wide:
        proj[:, :wcols] = dot_nt(tok[...], wall[...])
    else:
        def shard(i, carry):
            proj[:, :wcols] += dot_nt(tok[i], wall[i])
            return carry

        lax.fori_loop(0, n_dp, shard, 0)
    rate_scale = -jnp.exp(vec[0:1, :])
    b = proj[:, :STATE].astype(BF16)
    z = proj[:, STATE:STATE + LANES] + vec[1:2, :]
    dt = jnp.maximum(z, 0.0) + jnp.log1p(jnp.exp(-jnp.abs(z)))
    row_i, col_i = iota((t, t), 0), iota((t, t), 1)
    lower = jnp.where(row_i >= col_i, 1.0, 0.0).astype(BF16)
    upper = jnp.where(col_i >= row_i, 1.0, 0.0).astype(BF16)
    cum = dot_exact(lower, rate_scale * dt)
    cum_r[...] = cum
    dt_r[...] = dt
    cumt[...] = cum.T
    last = cum_r[t - 1:t, :]
    to_end = jnp.exp(last - cum)
    wgt = to_end * dt
    grow = jnp.exp(cum)
    w_bf = wgt.astype(BF16)
    e_bf = grow.astype(BF16)
    cv = c[...]
    bt = b.astype(F32).T.astype(BF16)
    ct = cv.astype(F32).T.astype(BF16)

    def spreader(q):
        return jnp.where(iota((LANES, LANES), 0) == gh * q + iota((LANES, LANES), 1) // width, 1.0, 0.0).astype(BF16)

    def gather_heads(q):
        return jnp.where(iota((LANES, LANES), 1) == gh * q + iota((LANES, LANES), 0) // width, 1.0, 0.0).astype(BF16)

    def summary(q, carry):
        e = spreader(q)
        xq = (dot(w_bf, e) * x[:, lanes(q)].astype(F32)).astype(BF16)
        gq = (dot(e_bf, e) * g[:, lanes(q)].astype(F32)).astype(BF16)
        xw[:, lanes(q)] = xq
        gwt[:, lanes(q)] = gq
        sloc[0, :, lanes(q)] = dot(bt, xq).astype(BF16)
        sloc[1, :, lanes(q)] = dot(ct, gq).astype(BF16)
        return carry

    lax.fori_loop(0, groups, summary, 0)
    each(n_ctx, lambda k: c_copy(k).start())
    if n_ctx > 2:
        decs[...] = jnp.broadcast_to(jnp.exp(last), decs.shape)
        crecv[my] = jnp.zeros(crecv.shape[1:], BF16)
        decr[my] = jnp.zeros(decr.shape[1:], F32)
        each(n_ctx, lambda k: d_copy(k).start())

    scores = dot_nt(b, cv)
    causal = col_i >= row_i

    def mix(q, carry):
        x4, g4 = x[:, lanes(q)], g[:, lanes(q)]
        head = iota((t, LANES), 1) // width
        zero = jnp.zeros_like(x4)
        xm = jnp.concatenate([jnp.where(head == j, x4, zero) for j in range(gh)], axis=0)
        d_all = dot_nt(xm, g4)
        shift = lax.rem(LANES - gh * q, LANES)
        cum_s = pltpu.roll(cum_r[...], shift, 1)
        dt_s = pltpu.roll(dt_r[...], shift, 1)
        total = ds[...]
        quot = qacc[...]
        mixed = []
        for j in range(gh):
            h = gh * q + j
            spread = cumt[pl.ds(h, 1), :] - cum_s[:, j:j + 1]
            factor = jnp.exp(jnp.where(causal, spread, -1e30))
            step = dt_s[:, j:j + 1]
            d = d_all[j * t:(j + 1) * t]
            fs = factor * scores
            mixed.append((fs * step).astype(BF16))
            u = d * fs
            quot = jnp.where(col_i == h, jnp.sum(u, axis=1, keepdims=True), quot)
            rowt[pl.ds(h, 1), :] = jnp.sum(u * step, axis=0, keepdims=True)
            total = total + d * (factor * step)
        ds[...] = total
        qacc[...] = quot
        out = dot(jnp.concatenate(mixed, axis=0), g4)
        acc = dexp[:, lanes(q)] * g4.astype(F32)
        for j in range(gh):
            acc = acc + jnp.where(head == j, out[j * t:(j + 1) * t], 0.0)
        dx[:, lanes(q)] = acc
        return carry

    rowt[...] = jnp.zeros_like(rowt)
    lax.fori_loop(0, groups, mix, 0)
    each(n_ctx, lambda k: c_copy(k).wait_recv())
    if n_ctx > 2:
        each(n_ctx, lambda k: d_copy(k).wait_recv())
        gs[...] = jnp.zeros_like(gs)

    def apply(q, carry):
        e, et = spreader(q), gather_heads(q)
        if n_ctx == 2:
            got = crecv[1 - my, :, lanes(q)]
            none = jnp.zeros_like(got)
            s4 = jnp.where(my > 0, got, none)
            g4s = jnp.where(my < 1, got, none)
        else:
            s = jnp.zeros((STATE, LANES), F32)
            for i in range(n_ctx):
                hi, mid = split(decr[i])
                dec = (dot(hi, e) + dot(mid, e))[0:1]
                s = jnp.where(i < my, dec * s + crecv[i, :, lanes(q)].astype(F32), s)
            k = jnp.zeros((STATE, LANES), F32)
            for i in reversed(range(n_ctx)):
                hi, mid = split(decr[i])
                dec = (dot(hi, e) + dot(mid, e))[0:1]
                k = jnp.where(i > my, dec * k + crecv[i, :, lanes(q)].astype(F32), k)
            s4, g4s = s.astype(BF16), k.astype(BF16)
            both = jnp.sum(s * k, axis=0, keepdims=True)
            gs[...] += dot_split(jnp.broadcast_to(both, (8, LANES)), et)
        us = dot(cv, s4)
        ug = dot(b, g4s)
        sv[...] += dot_split(x[:, lanes(q)].astype(F32) * ug, et)
        sg[...] += dot_split(g[:, lanes(q)].astype(F32) * us, et)
        db2[...] += dot_nt(xw[:, lanes(q)], g4s)
        dc2[...] += dot_nt(gwt[:, lanes(q)], s4)
        gx[:, lanes(q)] = (dx[:, lanes(q)] + dot(w_bf, e) * ug).astype(BF16)
        return carry

    lax.fori_loop(0, groups, apply, 0)
    dsv = ds[...]
    db = dot_split(dsv, cv) + db2[...]
    dc = dot_split(dsv.T, b) + dc2[...]
    gc[...] = dc.astype(BF16)
    quot = qacc[...]
    v = sv[...]
    vw = v * wgt
    dcum = rowt[...].T + grow * sg[...] - dt * quot - vw
    tail = jnp.sum(vw, axis=0, keepdims=True)
    if n_ctx > 2:
        tail = tail + jnp.exp(last) * gs[0:1, :]
    dcum = dcum + jnp.where(row_i == t - 1, tail, 0.0)
    drate = dot_exact(upper, dcum)
    ddt = quot + v * to_end + rate_scale * drate
    dz = ddt / (1.0 + jnp.exp(-z))
    proj[...] = jnp.zeros_like(proj)
    proj[:, :STATE] = db.astype(BF16).astype(F32)
    proj[:, STATE:cols] = dz[:, :heads]
    whole = proj[...]
    gpt[...] = whole.T[:wcols].astype(BF16)
    each(n_dp, lambda k: g_copy(k).start())
    gall[:, blk(me)] = gpt[...]
    gp[...] = whole[:, :cols].astype(BF16)
    each(n_dp, lambda k: a_copy(k).wait_recv())
    each(n_dp, lambda k: g_copy(k).wait_recv())
    part[...] = dot(gall[...], trecv[...])
    for o in range(n_ctx):
        pst[o] = part[o * cb:o * cb + cbp, :]
    each(n_ctx, lambda k: p_copy(k).start())
    each(n_ctx, lambda k: p_copy(k).wait_recv())

    def add(k, acc):
        return acc + precv[mate(k)]

    total = lax.fori_loop(1, n_ctx, add, pst[my])
    gw[...] = (total * (1.0 / n_dp)).T[:, :cb]
    each(n_dp, lambda k: w_copy(k).wait_send())
    each(n_dp, lambda k: a_copy(k).wait_send())
    each(n_dp, lambda k: g_copy(k).wait_send())
    each(n_ctx, lambda k: c_copy(k).wait_send())
    each(n_ctx, lambda k: p_copy(k).wait_send())
    if n_ctx > 2:
        each(n_ctx, lambda k: d_copy(k).wait_send())


def per_device(layer_in, inner_act, readout, w_in, a_log, dt_bias, d_skip, grad_out):
    n_dp, n_ctx = lax.axis_size("dp"), lax.axis_size("ctx")
    tokens, x, c, g = layer_in[0], inner_act[0], readout[0], grad_out[0]
    t, inner = x.shape
    rows, cols = w_in.shape
    heads = a_log.shape[0]
    width = inner // heads
    wcols = up(cols, 16)
    wide = rows % LANES == 0
    wt = jnp.pad(w_in.T, ((0, wcols - cols), (0, 0)))
    if not wide:
        tokens = jnp.swapaxes(tokens.reshape(t, n_dp, rows), 0, 1)
    vec = jnp.pad(jnp.stack([a_log, dt_bias]), ((0, 6), (0, LANES - heads)))
    dexp = jnp.repeat(d_skip, width)[None]
    cb = cols // n_ctx
    cbp = up(cb, 8)
    vm = pltpu.VMEM
    scratch = [
        vm((wcols, n_dp * rows) if wide else (n_dp, wcols, rows), BF16),
        vm((n_dp * t, rows), BF16),
        vm((wcols, n_dp * t), BF16),
        vm((2, STATE, inner), BF16),
        vm((n_ctx, STATE, inner), BF16),
        vm((8, LANES), BF16),
        vm((8, LANES), BF16),
        vm((t, inner), BF16),
        vm((t, inner), BF16),
        vm((t, inner), F32),
        vm((t, 2 * LANES), F32),
        vm((t, LANES), F32),
        vm((t, LANES), F32),
        vm((LANES, t), F32),
        vm((LANES, t), F32),
        vm((t, LANES), F32),
        vm((t, t), F32),
        vm((t, LANES), F32),
        vm((t, LANES), F32),
        vm((t, STATE), F32),
        vm((t, STATE), F32),
        vm((wcols, t), BF16),
        vm((wcols, rows), F32),
        vm((n_ctx, cbp, rows), F32),
        vm((n_ctx, cbp, rows), F32),
        vm((8, LANES), F32),
        vm((n_ctx, 8, LANES), F32),
        vm((8, LANES), F32),
    ]
    dma = pltpu.SemaphoreType.DMA
    scratch += [dma((n_dp,))] * 6 + [dma((n_ctx,))] * 6
    spec = pl.BlockSpec(memory_space=pltpu.VMEM)
    cfg = (n_dp, n_ctx, t, rows, heads, width, cols)
    gx, gc, gp, gw = pl.pallas_call(
        functools.partial(kernel, cfg),
        out_shape=(
            jax.ShapeDtypeStruct((t, inner), BF16),
            jax.ShapeDtypeStruct((t, STATE), BF16),
            jax.ShapeDtypeStruct((t, cols), BF16),
            jax.ShapeDtypeStruct((rows, cb), F32),
        ),
        in_specs=[spec] * 7,
        out_specs=(spec,) * 4,
        scratch_shapes=scratch,
        compiler_params=pltpu.CompilerParams(
            collective_id=0, has_side_effects=True, vmem_limit_bytes=48 * 1024 * 1024),
        name="ssm_backward",
    )(tokens, x, g, c, wt, vec, dexp)
    return (gx[None], gc[None], gp[None], gw)


def solution(mesh):
    in_specs = (
        P("dp", "ctx", None),
        P("dp", "ctx", None),
        P("dp", "ctx", None),
        P("dp", None),
        P(),
        P(),
        P(),
        P("dp", "ctx", None),
    )
    out_specs = (P("dp", "ctx", None), P("dp", "ctx", None), P("dp", "ctx", None), P("dp", "ctx"))
    return jax.shard_map(
        per_device, mesh=mesh, in_specs=in_specs, out_specs=out_specs, check_vma=False
    )
```

time: 215 us -> 85.3 us (0.40)
  the two profiles are of different devices: /device:TPU:0 before, /device:TPU:29 now
where the time goes in v1:
time: 85.3 us; the launch traced here: 85 us
  Pallas kernels  77 us (90%)
  local copies, waits for them, and re-layouts  6.57 us (8%)
    pallas_call x1, Pallas kernels, per_device(): pl.pallas_call(functools.partial(kernel, cfg), out_shape=(jax.ShapeDtypeS...  77 us
    unnamed x17, local copies, waits for them, and re-layouts  6.4 us

profile of v1, /device:TPU:29, one launch (start us, length us, event | category | flops | bytes accessed | tf_op | source)
XLA Modules:
  0.0 85.0 jit_solution(16617297720085774980)
XLA Ops:
  0.6 0.0 copy-start.4
  0.6 0.0 copy-start.5
  0.7 0.0 copy-start.3
  0.7 0.7 select_maximum_fusion.vec
  1.4 0.0 copy-done.4
  1.4 0.1 copy.16
  1.5 0.0 copy-done.5
  1.5 0.1 broadcast_in_dim.12
  1.6 0.1 broadcast_in_dim_reshape.3.dexp
  1.7 0.0 copy-done.3
  1.7 0.0 copy-start
  1.7 1.2 %copy-done = bf16[1,128,4096]{2,1,0:T(8,128)(2,1)S(1)} copy-done((bf16[1,128,4096]{2,1,0:T(8,128)(2,1)S(1)}, bf16[1,128,4096]{2,1,0:T(8,128)(2,1)}, u32[]{:S(2)}) %copy-start) | copy-done | bytes 1048600
  2.9 0.0 copy-start.1
  2.9 1.1 %copy-done.1 = bf16[1,128,2176]{2,1,0:T(8,128)(2,1)S(1)} copy-done((bf16[1,128,2176]{2,1,0:T(8,128)(2,1)S(1)}, bf16[1,128,2176]{2,1,0:T(8,128)(2,1)}, u32[]{:S(2)}) %copy-start.1) | copy-done | bytes 557080
  4.0 0.0 copy-start.2
  4.0 1.1 %copy-done.2 = bf16[1,128,2176]{2,1,0:T(8,128)(2,1)S(1)} copy-done((bf16[1,128,2176]{2,1,0:T(8,128)(2,1)S(1)}, bf16[1,128,2176]{2,1,0:T(8,128)(2,1)}, u32[]{:S(2)}) %copy-start.2) | copy-done | bytes 557080
  5.0 77.0 %ssm_backward.1 = (bf16[128,2176]{1,0:T(8,128)(2,1)S(1)}, bf16[128,64]{1,0:T(8,128)(2,1)S(1)}, bf16[128,132]{1,0:T(8,128)(2,1)S(1)}, f32[256,66]{1,0:T(8,128)S(1)}) custom-call(bf16[128,4096]{1,0:T(8,128)(2,1)S(1)} %bitcast.10, bf16[128,2176]{1,0:T(8,128)(2,1)S(1)} %bitcast.11, bf16[128,2176]{1,0:T(8,128)(2,1)S(1)} %bitcast.12, ...), custom_call_target="tpu_custom_call" | custom-call | tf_op jit(solution)/shard_map/ssm_backward/pallas_call | solution.py:368
  82.1 0.7 copy.17
  82.8 0.7 copy.18
  83.5 0.7 copy.19
  84.2 0.8 copy.21
  (1 shorter events, 0.0 us)
Async XLA Ops:
  0.6 0.7 copy-start.4
  0.6 0.9 %copy-start.5 = (f32[68]{0:T(128)S(1)}, f32[68]{0:T(128)}, u32[]{:S(2)}) copy-start(f32[68]{0:T(128)} %param.14) | copy-start | bytes 820
  0.7 1.0 %copy-start.3 = (bf16[256,132]{0,1:T(8,128)(2,1)S(1)}, bf16[256,132]{0,1:T(8,128)(2,1)}, u32[]{:S(2)}) copy-start(bf16[256,132]{0,1:T(8,128)(2,1)} %param.11) | copy-start | bytes 202756
  1.7 1.2 %copy-start = (bf16[1,128,4096]{2,1,0:T(8,128)(2,1)S(1)}, bf16[1,128,4096]{2,1,0:T(8,128)(2,1)}, u32[]{:S(2)}) copy-start(bf16[1,128,4096]{2,1,0:T(8,128)(2,1)} %param.8) | copy-start | bytes 3145732
  2.9 1.1 %copy-start.1 = (bf16[1,128,2176]{2,1,0:T(8,128)(2,1)S(1)}, bf16[1,128,2176]{2,1,0:T(8,128)(2,1)}, u32[]{:S(2)}) copy-start(bf16[1,128,2176]{2,1,0:T(8,128)(2,1)} %param.9) | copy-start | bytes 1671172
  4.0 1.1 %copy-start.2 = (bf16[1,128,2176]{2,1,0:T(8,128)(2,1)S(1)}, bf16[1,128,2176]{2,1,0:T(8,128)(2,1)}, u32[]{:S(2)}) copy-start(bf16[1,128,2176]{2,1,0:T(8,128)(2,1)} %param.15) | copy-start | bytes 1671172

commit v2 on v1

--- a/solution.py
+++ b/solution.py
@@ -14,6 +14,13 @@
 BF16 = jnp.bfloat16
 
 
+def inner_group(n):
+    b = 1
+    while b * b < n and n % (2 * b) == 0:
+        b *= 2
+    return b
+
+
 def up(n, m):
     return -(-n // m) * m
 
@@ -47,11 +54,19 @@
     return lax.broadcasted_iota(jnp.int32, shape, dim)
 
 
-def kernel(cfg, tok, x, g, c, w, vec, dexp, gx, gc, gp, gw, wall, trecv, gall, sloc, crecv, sin, gin,
-           xw, gwt, dx, proj, cum_r, dt_r, cumt, rowt, qacc, ds, sv, sg, db2, dc2, gpt, part, pst, precv,
-           decs, decr, gs, ws, wr, as_, ar, gsn, gr, cs, cr, ps, pr, es, er):
+def kernel(cfg, tok_h, x_h, g_h, c, w, vec, dexp, gx, gc, gp, gw, tok, x, g, wall, trecv, gall, sloc, crecv,
+           dall, spread_m, gather_m, xw, gwt, dx, proj, cum_r, dt_r, cumt, rowt, qacc, ds, part, pst, precv,
+           decs, decr, wzs, wzr, wfs, wfr, as_, ar, gzs, gzr, gfs, gfr, cs, cr, ps, pr, es, er, ms, mr, ls):
     n_dp, n_ctx, t, rows, heads, width, cols = cfg
     wide = rows % LANES == 0
+    halved = wide and rows % (n_ctx * LANES) == 0 and n_ctx == 2
+    half = rows // n_ctx
+    n_b = inner_group(n_dp)
+    n_a = n_dp // n_b
+    my_a, my_b = lax.div(lax.axis_index("dp"), n_b), lax.rem(lax.axis_index("dp"), n_b)
+    loads = [pltpu.make_async_copy(src, dst, ls.at[i]) for i, (src, dst) in enumerate(((x_h, x), (g_h, g), (tok_h, tok)))]
+    for load in loads:
+        load.start()
     groups = x.shape[1] // LANES
     gh = LANES // width
     cb = cols // n_ctx
@@ -88,20 +103,39 @@
     lax.fori_loop(1, n_ctx, greet_mate, 0)
     pl.semaphore_wait(barrier, n_dp + n_ctx - 2)
 
-    def w_copy(k):
-        return pltpu.make_async_remote_copy(
-            src_ref=w, dst_ref=col(wall, me), send_sem=ws.at[k], recv_sem=wr.at[k],
-            device_id=(peer(k), my), device_id_type=MESH)
+    def origin(ka, kb):
+        return lax.rem(my_a + n_a - ka, n_a) * n_b + lax.rem(my_b + n_b - kb, n_b)
+
+    def w_slot(i):
+        if halved:
+            return wall.at[my, :, pl.ds(pl.multiple_of(i * half, LANES), half)]
+        return col(wall, i)
+
+    def g_slot(i):
+        return gall.at[:, blk(i)]
+
+    def far(slot, send, recv, ka):
+        return pltpu.make_async_remote_copy(
+            src_ref=slot(me), dst_ref=slot(me), send_sem=send.at[ka], recv_sem=recv.at[ka],
+            device_id=(lax.rem(my_a + ka, n_a) * n_b + my_b, my), device_id_type=MESH)
+
+    def near(slot, send, recv, ka, kb):
+        i = origin(ka, 0)
+        return pltpu.make_async_remote_copy(
+            src_ref=slot(i), dst_ref=slot(i), send_sem=send.at[ka * n_b + kb], recv_sem=recv.at[ka * n_b + kb],
+            device_id=(my_a * n_b + lax.rem(my_b + kb, n_b), my), device_id_type=MESH)
+
+    def across(ka):
+        i = lax.rem(my_a + n_a - ka, n_a) * n_b
+        block = wall.at[my, :, pl.ds(pl.multiple_of(i * half, LANES), n_b * half)]
+        return pltpu.make_async_remote_copy(
+            src_ref=block, dst_ref=block, send_sem=ms.at[ka], recv_sem=mr.at[ka],
+            device_id=(me, 1 - my), device_id_type=MESH)
 
     def a_copy(k):
         return pltpu.make_async_remote_copy(
             src_ref=col(tok, peer(k)), dst_ref=trecv.at[blk(me), :], send_sem=as_.at[k],
             recv_sem=ar.at[k], device_id=(peer(k), my), device_id_type=MESH)
-
-    def g_copy(k):
-        return pltpu.make_async_remote_copy(
-            src_ref=gpt, dst_ref=gall.at[:, blk(me)], send_sem=gsn.at[k], recv_sem=gr.at[k],
-            device_id=(peer(k), my), device_id_type=MESH)
 
     def c_copy(k):
         other = mate(k)
@@ -127,22 +161,84 @@
 
         lax.fori_loop(1, n, step, 0)
 
-    each(n_dp, lambda k: w_copy(k).start())
+    def spread_near(slot, send, recv, ka):
+        each(n_b, lambda kb: near(slot, send, recv, ka, kb).start())
+
+    def first(slot, send, recv, fsend, frecv):
+        each(n_a, lambda ka: far(slot, send, recv, ka).start())
+        spread_near(slot, fsend, frecv, 0)
+
+    def pass_on(slot, send, recv, fsend, frecv):
+        def one(ka):
+            far(slot, send, recv, ka).wait_recv()
+            spread_near(slot, fsend, frecv, ka)
+
+        each(n_a, one)
+
+    def arrive(slot, fsend, frecv, ka):
+        each(n_b, lambda kb: near(slot, fsend, frecv, ka, kb).wait_recv())
+
+    def settle(slot, send, recv, fsend, frecv):
+        each(n_a, lambda ka: far(slot, send, recv, ka).wait_send())
+
+        def one(ka, carry):
+            each(n_b, lambda kb: near(slot, fsend, frecv, ka, kb).wait_send())
+            return carry
+
+        lax.fori_loop(0, n_a, one, 0)
+
+    inner = x.shape[1]
+    wcols = w.shape[0]
+    if halved:
+        wall[my, :, pl.ds(pl.multiple_of(me * half, LANES), half)] = w[:, pl.ds(pl.multiple_of(my * half, LANES), half)]
+    elif wide:
+        wall[:, pl.ds(pl.multiple_of(me * rows, LANES), rows)] = w[...]
+    else:
+        wall[me] = w[...]
+    first(w_slot, wzs, wzr, wfs, wfr)
+    loads[0].wait()
+    loads[1].wait()
+    loads[2].wait()
+    pass_on(w_slot, wzs, wzr, wfs, wfr)
+    each(n_dp, lambda k: a_copy(k).start())
     if wide:
-        wall[:, pl.ds(pl.multiple_of(me * rows, LANES), rows)] = w[...]
         trecv[blk(me), :] = tok[:, pl.ds(pl.multiple_of(me * rows, LANES), rows)]
     else:
-        wall[me] = w[...]
         trecv[blk(me), :] = tok[me]
     proj[...] = jnp.zeros_like(proj)
     qacc[...] = jnp.zeros_like(qacc)
     ds[...] = jnp.zeros_like(ds)
-    for ref in (sv, sg, db2, dc2):
-        ref[...] = jnp.zeros_like(ref)
-    each(n_dp, lambda k: w_copy(k).wait_recv())
-    each(n_dp, lambda k: a_copy(k).start())
-    wcols = w.shape[0]
-    if wide:
+    rowt[...] = jnp.zeros_like(rowt)
+    spread_m[...] = jnp.where(iota((LANES, inner), 0) == iota((LANES, inner), 1) // width, 1.0, 0.0).astype(BF16)
+    gather_m[...] = jnp.where(iota((inner, LANES), 1) == iota((inner, LANES), 0) // width, 1.0, 0.0).astype(BF16)
+    head = iota((t, LANES), 1) // width
+
+    def outer(q, carry):
+        x4 = x[:, lanes(q)]
+        zero = jnp.zeros_like(x4)
+        xm = jnp.concatenate([jnp.where(head == j, x4, zero) for j in range(gh)], axis=0)
+        dall[q] = dot_nt(xm, g[:, lanes(q)])
+        return carry
+
+    lax.fori_loop(0, groups, outer, 0)
+
+    def land(ka, carry):
+        arrive(w_slot, wfs, wfr, ka)
+        if halved:
+            across(ka).start()
+        return carry
+
+    lax.fori_loop(0, n_a, land, 0)
+    if halved:
+        lax.fori_loop(0, n_a, lambda ka, carry: (across(ka).wait_recv(), carry)[1], 0)
+        total = None
+        for k in range(n_ctx):
+            picked = jnp.concatenate(
+                [tok[:, i * rows + k * half:i * rows + (k + 1) * half] for i in range(n_dp)], axis=1)
+            term = dot_nt(picked, wall[k])
+            total = term if total is None else total + term
+        proj[:, :wcols] = total
+    elif wide:
         proj[:, :wcols] = dot_nt(tok[...], wall[...])
     else:
         def shard(i, carry):
@@ -171,23 +267,12 @@
     bt = b.astype(F32).T.astype(BF16)
     ct = cv.astype(F32).T.astype(BF16)
 
-    def spreader(q):
-        return jnp.where(iota((LANES, LANES), 0) == gh * q + iota((LANES, LANES), 1) // width, 1.0, 0.0).astype(BF16)
-
-    def gather_heads(q):
-        return jnp.where(iota((LANES, LANES), 1) == gh * q + iota((LANES, LANES), 0) // width, 1.0, 0.0).astype(BF16)
-
-    def summary(q, carry):
-        e = spreader(q)
-        xq = (dot(w_bf, e) * x[:, lanes(q)].astype(F32)).astype(BF16)
-        gq = (dot(e_bf, e) * g[:, lanes(q)].astype(F32)).astype(BF16)
-        xw[:, lanes(q)] = xq
-        gwt[:, lanes(q)] = gq
-        sloc[0, :, lanes(q)] = dot(bt, xq).astype(BF16)
-        sloc[1, :, lanes(q)] = dot(ct, gq).astype(BF16)
-        return carry
-
-    lax.fori_loop(0, groups, summary, 0)
+    span = [slice(q * LANES, (q + 1) * LANES) for q in range(groups)]
+    for at in span:
+        xw[:, at] = (dot(w_bf, spread_m[:, at]) * x[:, at].astype(F32)).astype(BF16)
+        gwt[:, at] = (dot(e_bf, spread_m[:, at]) * g[:, at].astype(F32)).astype(BF16)
+    sloc[0] = dot(bt, xw[...]).astype(BF16)
+    sloc[1] = dot(ct, gwt[...]).astype(BF16)
     each(n_ctx, lambda k: c_copy(k).start())
     if n_ctx > 2:
         decs[...] = jnp.broadcast_to(jnp.exp(last), decs.shape)
@@ -199,11 +284,7 @@
     causal = col_i >= row_i
 
     def mix(q, carry):
-        x4, g4 = x[:, lanes(q)], g[:, lanes(q)]
-        head = iota((t, LANES), 1) // width
-        zero = jnp.zeros_like(x4)
-        xm = jnp.concatenate([jnp.where(head == j, x4, zero) for j in range(gh)], axis=0)
-        d_all = dot_nt(xm, g4)
+        g4 = g[:, lanes(q)]
         shift = lax.rem(LANES - gh * q, LANES)
         cum_s = pltpu.roll(cum_r[...], shift, 1)
         dt_s = pltpu.roll(dt_r[...], shift, 1)
@@ -215,7 +296,7 @@
             spread = cumt[pl.ds(h, 1), :] - cum_s[:, j:j + 1]
             factor = jnp.exp(jnp.where(causal, spread, -1e30))
             step = dt_s[:, j:j + 1]
-            d = d_all[j * t:(j + 1) * t]
+            d = dall[q, j * t:(j + 1) * t]
             fs = factor * scores
             mixed.append((fs * step).astype(BF16))
             u = d * fs
@@ -231,52 +312,48 @@
         dx[:, lanes(q)] = acc
         return carry
 
-    rowt[...] = jnp.zeros_like(rowt)
     lax.fori_loop(0, groups, mix, 0)
     each(n_ctx, lambda k: c_copy(k).wait_recv())
     if n_ctx > 2:
         each(n_ctx, lambda k: d_copy(k).wait_recv())
-        gs[...] = jnp.zeros_like(gs)
-
-    def apply(q, carry):
-        e, et = spreader(q), gather_heads(q)
+
+    sv = sg = jnp.zeros((t, LANES), F32)
+    db2 = dc2 = jnp.zeros((t, STATE), F32)
+    gs = jnp.zeros((8, LANES), F32)
+    for at in span:
+        e, et = spread_m[:, at], gather_m[at, :]
         if n_ctx == 2:
-            got = crecv[1 - my, :, lanes(q)]
+            got = crecv[1 - my, :, at]
             none = jnp.zeros_like(got)
             s4 = jnp.where(my > 0, got, none)
             g4s = jnp.where(my < 1, got, none)
         else:
             s = jnp.zeros((STATE, LANES), F32)
+            k = s
             for i in range(n_ctx):
-                hi, mid = split(decr[i])
-                dec = (dot(hi, e) + dot(mid, e))[0:1]
-                s = jnp.where(i < my, dec * s + crecv[i, :, lanes(q)].astype(F32), s)
-            k = jnp.zeros((STATE, LANES), F32)
+                dec = dot_split(decr[i], e)[0:1]
+                s = jnp.where(i < my, dec * s + crecv[i, :, at].astype(F32), s)
             for i in reversed(range(n_ctx)):
-                hi, mid = split(decr[i])
-                dec = (dot(hi, e) + dot(mid, e))[0:1]
-                k = jnp.where(i > my, dec * k + crecv[i, :, lanes(q)].astype(F32), k)
+                dec = dot_split(decr[i], e)[0:1]
+                k = jnp.where(i > my, dec * k + crecv[i, :, at].astype(F32), k)
             s4, g4s = s.astype(BF16), k.astype(BF16)
             both = jnp.sum(s * k, axis=0, keepdims=True)
-            gs[...] += dot_split(jnp.broadcast_to(both, (8, LANES)), et)
+            gs = gs + dot_split(jnp.broadcast_to(both, (8, LANES)), et)
         us = dot(cv, s4)
         ug = dot(b, g4s)
-        sv[...] += dot_split(x[:, lanes(q)].astype(F32) * ug, et)
-        sg[...] += dot_split(g[:, lanes(q)].astype(F32) * us, et)
-        db2[...] += dot_nt(xw[:, lanes(q)], g4s)
-        dc2[...] += dot_nt(gwt[:, lanes(q)], s4)
-        gx[:, lanes(q)] = (dx[:, lanes(q)] + dot(w_bf, e) * ug).astype(BF16)
-        return carry
-
-    lax.fori_loop(0, groups, apply, 0)
+        sv = sv + dot_split(x[:, at].astype(F32) * ug, et)
+        sg = sg + dot_split(g[:, at].astype(F32) * us, et)
+        db2 = db2 + dot_nt(xw[:, at], g4s)
+        dc2 = dc2 + dot_nt(gwt[:, at], s4)
+        gx[:, at] = (dx[:, at] + dot(w_bf, e) * ug).astype(BF16)
     dsv = ds[...]
-    db = dot_split(dsv, cv) + db2[...]
-    dc = dot_split(dsv.T, b) + dc2[...]
+    db = dot_split(dsv, cv) + db2
+    dc = dot_split(dsv.T, b) + dc2
     gc[...] = dc.astype(BF16)
     quot = qacc[...]
-    v = sv[...]
+    v = sv
     vw = v * wgt
-    dcum = rowt[...].T + grow * sg[...] - dt * quot - vw
+    dcum = rowt[...].T + grow * sg - dt * quot - vw
     tail = jnp.sum(vw, axis=0, keepdims=True)
     if n_ctx > 2:
         tail = tail + jnp.exp(last) * gs[0:1, :]
@@ -288,12 +365,12 @@
     proj[:, :STATE] = db.astype(BF16).astype(F32)
     proj[:, STATE:cols] = dz[:, :heads]
     whole = proj[...]
-    gpt[...] = whole.T[:wcols].astype(BF16)
-    each(n_dp, lambda k: g_copy(k).start())
-    gall[:, blk(me)] = gpt[...]
+    gall[:, blk(me)] = whole.T[:wcols].astype(BF16)
+    first(g_slot, gzs, gzr, gfs, gfr)
     gp[...] = whole[:, :cols].astype(BF16)
+    pass_on(g_slot, gzs, gzr, gfs, gfr)
     each(n_dp, lambda k: a_copy(k).wait_recv())
-    each(n_dp, lambda k: g_copy(k).wait_recv())
+    lax.fori_loop(0, n_a, lambda ka, carry: (arrive(g_slot, gfs, gfr, ka), carry)[1], 0)
     part[...] = dot(gall[...], trecv[...])
     for o in range(n_ctx):
         pst[o] = part[o * cb:o * cb + cbp, :]
@@ -305,13 +382,24 @@
 
     total = lax.fori_loop(1, n_ctx, add, pst[my])
     gw[...] = (total * (1.0 / n_dp)).T[:, :cb]
-    each(n_dp, lambda k: w_copy(k).wait_send())
+    settle(w_slot, wzs, wzr, wfs, wfr)
+    if halved:
+        lax.fori_loop(0, n_a, lambda ka, carry: (across(ka).wait_send(), carry)[1], 0)
     each(n_dp, lambda k: a_copy(k).wait_send())
-    each(n_dp, lambda k: g_copy(k).wait_send())
+    settle(g_slot, gzs, gzr, gfs, gfr)
     each(n_ctx, lambda k: c_copy(k).wait_send())
     each(n_ctx, lambda k: p_copy(k).wait_send())
     if n_ctx > 2:
         each(n_ctx, lambda k: d_copy(k).wait_send())
+
+
+def store(*refs):
+    sems = refs[-1]
+    copies = [pltpu.make_async_copy(refs[i], refs[4 + i], sems.at[i]) for i in range(4)]
+    for copy in copies:
+        copy.start()
+    for copy in copies:
+        copy.wait()
 
 
 def per_device(layer_in, inner_act, readout, w_in, a_log, dt_bias, d_skip, grad_out):
@@ -331,14 +419,25 @@
     cb = cols // n_ctx
     cbp = up(cb, 8)
     vm = pltpu.VMEM
+    n_a = n_dp // inner_group(n_dp)
+    if not wide:
+        wall = (n_dp, wcols, rows)
+    elif rows % (n_ctx * LANES) == 0 and n_ctx == 2:
+        wall = (n_ctx, wcols, n_dp * rows // n_ctx)
+    else:
+        wall = (wcols, n_dp * rows)
     scratch = [
-        vm((wcols, n_dp * rows) if wide else (n_dp, wcols, rows), BF16),
+        vm(tokens.shape, BF16),
+        vm((t, inner), BF16),
+        vm((t, inner), BF16),
+        vm(wall, BF16),
         vm((n_dp * t, rows), BF16),
         vm((wcols, n_dp * t), BF16),
         vm((2, STATE, inner), BF16),
         vm((n_ctx, STATE, inner), BF16),
-        vm((8, LANES), BF16),
-        vm((8, LANES), BF16),
+        vm((inner // LANES, LANES // width * t, t), F32),
+        vm((LANES, inner), BF16),
+        vm((inner, LANES), BF16),
         vm((t, inner), BF16),
         vm((t, inner), BF16),
         vm((t, inner), F32),
@@ -349,23 +448,19 @@
         vm((LANES, t), F32),
         vm((t, LANES), F32),
         vm((t, t), F32),
-        vm((t, LANES), F32),
-        vm((t, LANES), F32),
-        vm((t, STATE), F32),
-        vm((t, STATE), F32),
-        vm((wcols, t), BF16),
         vm((wcols, rows), F32),
         vm((n_ctx, cbp, rows), F32),
         vm((n_ctx, cbp, rows), F32),
         vm((8, LANES), F32),
         vm((n_ctx, 8, LANES), F32),
-        vm((8, LANES), F32),
     ]
     dma = pltpu.SemaphoreType.DMA
-    scratch += [dma((n_dp,))] * 6 + [dma((n_ctx,))] * 6
+    scratch += [dma((n_a,))] * 2 + [dma((n_dp,))] * 4 + [dma((n_a,))] * 2 + [dma((n_dp,))] * 2
+    scratch += [dma((n_ctx,))] * 6 + [dma((n_a,))] * 2 + [dma((3,))]
+    hbm = pl.BlockSpec(memory_space=pltpu.HBM)
     spec = pl.BlockSpec(memory_space=pltpu.VMEM)
     cfg = (n_dp, n_ctx, t, rows, heads, width, cols)
-    gx, gc, gp, gw = pl.pallas_call(
+    results = pl.pallas_call(
         functools.partial(kernel, cfg),
         out_shape=(
             jax.ShapeDtypeStruct((t, inner), BF16),
@@ -373,13 +468,21 @@
             jax.ShapeDtypeStruct((t, cols), BF16),
             jax.ShapeDtypeStruct((rows, cb), F32),
         ),
-        in_specs=[spec] * 7,
+        in_specs=[hbm] * 3 + [spec] * 4,
         out_specs=(spec,) * 4,
         scratch_shapes=scratch,
         compiler_params=pltpu.CompilerParams(
             collective_id=0, has_side_effects=True, vmem_limit_bytes=48 * 1024 * 1024),
         name="ssm_backward",
     )(tokens, x, g, c, wt, vec, dexp)
+    gx, gc, gp, gw = pl.pallas_call(
+        store,
+        out_shape=tuple(jax.ShapeDtypeStruct(r.shape, r.dtype) for r in results),
+        in_specs=[spec] * 4,
+        out_specs=(hbm,) * 4,
+        scratch_shapes=[dma((4,))],
+        name="store_results",
+    )(*results)
     return (gx[None], gc[None], gp[None], gw)
 
 

time: 85.3 us -> 64.4 us (0.75)
  the two profiles are of different devices: /device:TPU:29 before, /device:TPU:0 now
where the time goes in v2:
time: 64.4 us; the launch traced here: 64.1 us
  Pallas kernels  52.5 us (82%)
  local copies, waits for them, and re-layouts  10.1 us (16%)
  between operations  0.74 us (1%)
  other arithmetic  0.71 us (1%)
    pallas_call x1, Pallas kernels, per_device(): pl.pallas_call(functools.partial(kernel, cfg), out_shape=(jax.ShapeDtypeS...  50.5 us
    unnamed x26, local copies, waits for them, and re-layouts  9.91 us
    pallas_call x1, Pallas kernels, per_device(): pl.pallas_call(store, out_shape=tuple((jax.ShapeDtypeStruct(r.shape, r.dt...  2.01 us

profile of v2, /device:TPU:0, one launch (start us, length us, event | category | flops | bytes accessed | tf_op | source)
XLA Modules:
  0.0 64.1 jit_solution(994207007976806090)
XLA Ops:
  0.6 0.0 copy-start.9
  0.6 0.0 copy-start.10
  0.7 0.0 copy-start.8
  0.7 0.7 %select_maximum_fusion.vec = f32[8,128]{1,0:T(8,128)S(1)} fusion(f32[1,68]{1,0:T(1,128)} %bitcast.17, f32[1,68]{1,0:T(1,128)} %bitcast.18), kind=kLoop, calls=%fused_computation | loop fusion | flops 8192 | bytes 4640 | tf_op jit(solution)/shard_map/stack | solution.py:417
  1.4 0.0 copy-done.9
  1.4 0.1 copy.16
  1.5 0.0 copy-done.10
  1.5 0.1 broadcast_in_dim.12
  1.6 0.1 broadcast_in_dim_reshape.3.dexp
  1.7 0.0 copy-done.8
  1.7 0.0 copy-start
  1.7 1.2 %copy-done = bf16[1,128,4096]{2,1,0:T(8,128)(2,1)S(1)} copy-done((bf16[1,128,4096]{2,1,0:T(8,128)(2,1)S(1)}, bf16[1,128,4096]{2,1,0:T(8,128)(2,1)}, u32[]{:S(2)}) %copy-start) | copy-done | bytes 1048600
  2.9 0.0 copy-start.1
  2.9 1.1 %copy-done.1 = bf16[1,128,2176]{2,1,0:T(8,128)(2,1)S(1)} copy-done((bf16[1,128,2176]{2,1,0:T(8,128)(2,1)S(1)}, bf16[1,128,2176]{2,1,0:T(8,128)(2,1)}, u32[]{:S(2)}) %copy-start.1) | copy-done | bytes 557080
  4.0 0.0 copy-start.2
  4.0 1.1 %copy-done.2 = bf16[1,128,2176]{2,1,0:T(8,128)(2,1)S(1)} copy-done((bf16[1,128,2176]{2,1,0:T(8,128)(2,1)S(1)}, bf16[1,128,2176]{2,1,0:T(8,128)(2,1)}, u32[]{:S(2)}) %copy-start.2) | copy-done | bytes 557080
  5.0 50.5 %ssm_backward.1 = (bf16[128,2176]{1,0:T(8,128)(2,1)S(1)}, bf16[128,64]{1,0:T(8,128)(2,1)S(1)}, bf16[128,132]{1,0:T(8,128)(2,1)S(1)}, f32[256,66]{1,0:T(8,128)S(1)}) custom-call(bf16[128,4096]{1,0:T(8,128)(2,1)S(1)} %bitcast.10, bf16[128,2176]{1,0:T(8,128)(2,1)S(1)} %bitcast.11, bf16[128,2176]{1,0:T(8,128)(2,1)S(1)} %bitcast.12, ...), custom_call_target="tpu_custom_call" | custom-call | tf_op jit(solution)/shard_map/ssm_backward/pallas_call | solution.py:463
  55.6 0.0 copy-start.3
  55.6 0.8 %copy-done.3 = bf16[128,2176]{1,0:T(8,128)(2,1)} copy-done((bf16[128,2176]{1,0:T(8,128)(2,1)}, bf16[128,2176]{1,0:T(8,128)(2,1)S(1)}, u32[]{:S(2)}) %copy-start.3) | copy-done | bytes 557080
  56.4 0.0 copy-start.4
  56.4 0.6 %copy-done.4 = f32[256,66]{1,0:T(8,128)} copy-done((f32[256,66]{1,0:T(8,128)}, f32[256,66]{1,0:T(8,128)S(1)}, u32[]{:S(2)}) %copy-start.4) | copy-done | bytes 67608
  57.0 0.0 copy-start.5
  57.0 0.6 copy-done.5
  57.6 0.0 copy-start.6
  57.6 0.6 copy-done.6
  58.3 2.0 %store_results.1 = (bf16[128,2176]{1,0:T(8,128)(2,1)}, bf16[128,64]{1,0:T(8,128)(2,1)}, bf16[128,132]{1,0:T(8,128)(2,1)}, f32[256,66]{1,0:T(8,128)}) custom-call(bf16[128,2176]{1,0:T(8,128)(2,1)} %copy-done.3, bf16[128,64]{1,0:T(8,128)(2,1)} %copy-done.6, bf16[128,132]{1,0:T(8,128)(2,1)} %copy-done.5, f32[256,66]{1,0:T(8,128)} %copy-done.4), custom_call_target="tpu_custom_call" | custom-call | tf_op jit(solution)/shard_map/store_results/pallas_call | solution.py:478
  60.3 0.0 copy-start.7
  60.3 1.5 %copy.17 = bf16[1,128,64]{1,2,0:T(8,128)(2,1)} copy(bf16[1,128,64]{2,1,0:T(8,128)(2,1)} %bitcast.16) | data formatting | bytes 32768
  61.8 1.6 %copy.18 = bf16[1,128,132]{1,2,0:T(8,128)(2,1)} copy(bf16[1,128,132]{2,1,0:T(8,128)(2,1)} %bitcast.15) | data formatting | bytes 67584
  63.3 0.0 copy-done.7
  63.3 0.7 %copy.19 = f32[256,66]{0,1:T(8,128)} copy(f32[256,66]{1,0:T(8,128)S(1)} %copy-done.7) | data formatting | bytes 135168
  (1 shorter events, 0.0 us)
Async XLA Ops:
  0.6 0.7 %copy-start.9 = (bf16[1,128,64]{1,2,0:T(8,128)(2,1)S(1)}, bf16[1,128,64]{1,2,0:T(8,128)(2,1)}, u32[]{:S(2)}) copy-start(bf16[1,128,64]{1,2,0:T(8,128)(2,1)} %param.10) | copy-start | bytes 49156
  0.6 0.9 %copy-start.10 = (f32[68]{0:T(128)S(1)}, f32[68]{0:T(128)}, u32[]{:S(2)}) copy-start(f32[68]{0:T(128)} %param.14) | copy-start | bytes 820
  0.7 1.0 %copy-start.8 = (bf16[256,132]{0,1:T(8,128)(2,1)S(1)}, bf16[256,132]{0,1:T(8,128)(2,1)}, u32[]{:S(2)}) copy-start(bf16[256,132]{0,1:T(8,128)(2,1)} %param.11) | copy-start | bytes 202756
  1.7 1.2 %copy-start = (bf16[1,128,4096]{2,1,0:T(8,128)(2,1)S(1)}, bf16[1,128,4096]{2,1,0:T(8,128)(2,1)}, u32[]{:S(2)}) copy-start(bf16[1,128,4096]{2,1,0:T(8,128)(2,1)} %param.8) | copy-start | bytes 3145732
  2.9 1.1 %copy-start.1 = (bf16[1,128,2176]{2,1,0:T(8,128)(2,1)S(1)}, bf16[1,128,2176]{2,1,0:T(8,128)(2,1)}, u32[]{:S(2)}) copy-start(bf16[1,128,2176]{2,1,0:T(8,128)(2,1)} %param.9) | copy-start | bytes 1671172
  4.0 1.1 %copy-start.2 = (bf16[1,128,2176]{2,1,0:T(8,128)(2,1)S(1)}, bf16[1,128,2176]{2,1,0:T(8,128)(2,1)}, u32[]{:S(2)}) copy-start(bf16[1,128,2176]{2,1,0:T(8,128)(2,1)} %param.15) | copy-start | bytes 1671172
  55.6 0.8 %copy-start.3 = (bf16[128,2176]{1,0:T(8,128)(2,1)}, bf16[128,2176]{1,0:T(8,128)(2,1)S(1)}, u32[]{:S(2)}) copy-start(bf16[128,2176]{1,0:T(8,128)(2,1)S(1)} %get-tuple-element.12.refs_0_) | copy-start | bytes 1671172
  56.4 0.6 %copy-start.4 = (f32[256,66]{1,0:T(8,128)}, f32[256,66]{1,0:T(8,128)S(1)}, u32[]{:S(2)}) copy-start(f32[256,66]{1,0:T(8,128)S(1)} %get-tuple-element.15.refs_3_) | copy-start | bytes 202756
  57.0 0.6 copy-start.5
  57.6 0.6 copy-start.6
  60.3 3.1 %copy-start.7 = (f32[256,66]{1,0:T(8,128)S(1)}, f32[256,66]{1,0:T(8,128)}, u32[]{:S(2)}) copy-start(f32[256,66]{1,0:T(8,128)} %get-tuple-element.27) | copy-start | bytes 202756

commit v3 on v2

--- a/solution.py
+++ b/solution.py
@@ -54,11 +54,12 @@
     return lax.broadcasted_iota(jnp.int32, shape, dim)
 
 
-def kernel(cfg, tok_h, x_h, g_h, c, w, vec, dexp, gx, gc, gp, gw, tok, x, g, wall, trecv, gall, sloc, crecv,
-           dall, spread_m, gather_m, xw, gwt, dx, proj, cum_r, dt_r, cumt, rowt, qacc, ds, part, pst, precv,
-           decs, decr, wzs, wzr, wfs, wfr, as_, ar, gzs, gzr, gfs, gfr, cs, cr, ps, pr, es, er, ms, mr, ls):
+def kernel(cfg, tok_h, x_h, g_h, c, w_own, a_log, dt_bias, d_skip, gx_h, gc_h, gp_h, gw_h, gx, gc, gp, gw, w, vec, tok, x, g, wall, trecv, gall, sloc, crecv,
+           dall, spread_m, gather_m, xw, gwt, dx, proj, cum_r, dt_r, cumt, rowt, qacc, ds, part, pst, precv, zst, zrecv,
+           decs, decr, wzs, wzr, wfs, wfr, as_, ar, gzs, gzr, gfs, gfr, os, cs, cr, ps, pr, es, er, ms, mr, ls):
     n_dp, n_ctx, t, rows, heads, width, cols = cfg
     wide = rows % LANES == 0
+    unroll = True
     halved = wide and rows % (n_ctx * LANES) == 0 and n_ctx == 2
     half = rows // n_ctx
     n_b = inner_group(n_dp)
@@ -70,7 +71,7 @@
     groups = x.shape[1] // LANES
     gh = LANES // width
     cb = cols // n_ctx
-    cbp = up(cb, 8)
+    cbp = up(cb, 16)
     me = lax.axis_index("dp")
     my = lax.axis_index("ctx")
 
@@ -112,7 +113,7 @@
         return col(wall, i)
 
     def g_slot(i):
-        return gall.at[:, blk(i)]
+        return gall.at[:, blk(lax.rem(i, n_b))]
 
     def far(slot, send, recv, ka):
         return pltpu.make_async_remote_copy(
@@ -132,10 +133,25 @@
             src_ref=block, dst_ref=block, send_sem=ms.at[ka], recv_sem=mr.at[ka],
             device_id=(me, 1 - my), device_id_type=MESH)
 
-    def a_copy(k):
-        return pltpu.make_async_remote_copy(
-            src_ref=col(tok, peer(k)), dst_ref=trecv.at[blk(me), :], send_sem=as_.at[k],
-            recv_sem=ar.at[k], device_id=(peer(k), my), device_id_type=MESH)
+    def a_copy(kb, a):
+        b_to = lax.rem(my_b + kb, n_b)
+        return pltpu.make_async_remote_copy(
+            src_ref=col(tok, a * n_b + b_to), dst_ref=trecv.at[a, blk(my_b), :],
+            send_sem=as_.at[kb * n_a + a], recv_sem=ar.at[kb * n_a + a],
+            device_id=(my_a * n_b + b_to, my), device_id_type=MESH)
+
+    def a_each(act):
+        def one(a, carry):
+            each(n_b, lambda kb: act(a_copy(kb, a)))
+            return carry
+
+        lax.fori_loop(0, n_a, one, 0)
+
+    def z_copy(k):
+        a_to = lax.rem(my_a + k, n_a)
+        return pltpu.make_async_remote_copy(
+            src_ref=zst.at[a_to], dst_ref=zrecv.at[my_a], send_sem=gzs.at[k], recv_sem=gzr.at[k],
+            device_id=(a_to * n_b + my_b, my), device_id_type=MESH)
 
     def c_copy(k):
         other = mate(k)
@@ -189,6 +205,8 @@
 
     inner = x.shape[1]
     wcols = w.shape[0]
+    w[...] = jnp.zeros_like(w)
+    w[:cols, :] = w_own[...]
     if halved:
         wall[my, :, pl.ds(pl.multiple_of(me * half, LANES), half)] = w[:, pl.ds(pl.multiple_of(my * half, LANES), half)]
     elif wide:
@@ -196,15 +214,15 @@
     else:
         wall[me] = w[...]
     first(w_slot, wzs, wzr, wfs, wfr)
-    loads[0].wait()
-    loads[1].wait()
-    loads[2].wait()
+    vec[...] = jnp.zeros_like(vec)
+    for i, ref in enumerate((a_log, dt_bias, d_skip)):
+        vec[i:i + 1, :heads] = ref[...]
+    for load in loads:
+        load.wait()
     pass_on(w_slot, wzs, wzr, wfs, wfr)
-    each(n_dp, lambda k: a_copy(k).start())
-    if wide:
-        trecv[blk(me), :] = tok[:, pl.ds(pl.multiple_of(me * rows, LANES), rows)]
-    else:
-        trecv[blk(me), :] = tok[me]
+    a_each(lambda copy: copy.start())
+    for a in range(n_a):
+        trecv[a, blk(my_b), :] = col(tok, a * n_b + my_b)[...]
     proj[...] = jnp.zeros_like(proj)
     qacc[...] = jnp.zeros_like(qacc)
     ds[...] = jnp.zeros_like(ds)
@@ -263,9 +281,10 @@
     grow = jnp.exp(cum)
     w_bf = wgt.astype(BF16)
     e_bf = grow.astype(BF16)
-    cv = c[...]
+    ct = c[...]
     bt = b.astype(F32).T.astype(BF16)
-    ct = cv.astype(F32).T.astype(BF16)
+    cv = ct.astype(F32).T.astype(BF16)
+    skip_hi, skip_lo = split(vec[...])
 
     span = [slice(q * LANES, (q + 1) * LANES) for q in range(groups)]
     for at in span:
@@ -306,13 +325,14 @@
         ds[...] = total
         qacc[...] = quot
         out = dot(jnp.concatenate(mixed, axis=0), g4)
-        acc = dexp[:, lanes(q)] * g4.astype(F32)
+        skip = dot(skip_hi, spread_m[:, lanes(q)]) + dot(skip_lo, spread_m[:, lanes(q)])
+        acc = skip[2:3] * g4.astype(F32)
         for j in range(gh):
             acc = acc + jnp.where(head == j, out[j * t:(j + 1) * t], 0.0)
         dx[:, lanes(q)] = acc
         return carry
 
-    lax.fori_loop(0, groups, mix, 0)
+    lax.fori_loop(0, groups, mix, 0, unroll=unroll)
     each(n_ctx, lambda k: c_copy(k).wait_recv())
     if n_ctx > 2:
         each(n_ctx, lambda k: d_copy(k).wait_recv())
@@ -346,10 +366,14 @@
         db2 = db2 + dot_nt(xw[:, at], g4s)
         dc2 = dc2 + dot_nt(gwt[:, at], s4)
         gx[:, at] = (dx[:, at] + dot(w_bf, e) * ug).astype(BF16)
+    stores = [pltpu.make_async_copy(src, dst, os.at[i]) for i, (src, dst) in enumerate(
+        ((gx, gx_h), (gc, gc_h), (gp, gp_h), (gw, gw_h)))]
+    stores[0].start()
     dsv = ds[...]
     db = dot_split(dsv, cv) + db2
     dc = dot_split(dsv.T, b) + dc2
-    gc[...] = dc.astype(BF16)
+    gc[...] = dc.T.astype(BF16)
+    stores[1].start()
     quot = qacc[...]
     v = sv
     vw = v * wgt
@@ -365,28 +389,38 @@
     proj[:, :STATE] = db.astype(BF16).astype(F32)
     proj[:, STATE:cols] = dz[:, :heads]
     whole = proj[...]
-    gall[:, blk(me)] = whole.T[:wcols].astype(BF16)
-    first(g_slot, gzs, gzr, gfs, gfr)
-    gp[...] = whole[:, :cols].astype(BF16)
-    pass_on(g_slot, gzs, gzr, gfs, gfr)
-    each(n_dp, lambda k: a_copy(k).wait_recv())
-    lax.fori_loop(0, n_a, lambda ka, carry: (arrive(g_slot, gfs, gfr, ka), carry)[1], 0)
-    part[...] = dot(gall[...], trecv[...])
-    for o in range(n_ctx):
-        pst[o] = part[o * cb:o * cb + cbp, :]
+    turned = whole.T[:wcols].astype(BF16)
+    gall[:, blk(my_b)] = turned
+    spread_near(g_slot, gfs, gfr, 0)
+    gp[...] = turned[:cols]
+    stores[2].start()
+    part[...] = jnp.zeros_like(part)
+    a_each(lambda copy: copy.wait_recv())
+    arrive(g_slot, gfs, gfr, 0)
+    for a in range(n_a):
+        part[a, :wcols] = dot(gall[...], trecv[a])
+        for o in range(n_ctx):
+            pst[o, a] = part[a, o * cb:o * cb + cbp, :].astype(BF16)
     each(n_ctx, lambda k: p_copy(k).start())
     each(n_ctx, lambda k: p_copy(k).wait_recv())
 
-    def add(k, acc):
-        return acc + precv[mate(k)]
-
-    total = lax.fori_loop(1, n_ctx, add, pst[my])
-    gw[...] = (total * (1.0 / n_dp)).T[:, :cb]
+    for a in range(n_a):
+        zst[a] = lax.fori_loop(
+            1, n_ctx, lambda k, acc: acc + precv[mate(k), a].astype(F32), pst[my, a].astype(F32)).astype(BF16)
+    each(n_a, lambda k: z_copy(k).start())
+    each(n_a, lambda k: z_copy(k).wait_recv())
+    total = lax.fori_loop(
+        1, n_a, lambda k, acc: acc + zrecv[lax.rem(my_a + k, n_a)].astype(F32), zst[my_a].astype(F32))
+    gw[...] = (total * (1.0 / n_dp))[:cb]
+    stores[3].start()
     settle(w_slot, wzs, wzr, wfs, wfr)
     if halved:
         lax.fori_loop(0, n_a, lambda ka, carry: (across(ka).wait_send(), carry)[1], 0)
-    each(n_dp, lambda k: a_copy(k).wait_send())
-    settle(g_slot, gzs, gzr, gfs, gfr)
+    a_each(lambda copy: copy.wait_send())
+    each(n_b, lambda kb: near(g_slot, gfs, gfr, 0, kb).wait_send())
+    each(n_a, lambda k: z_copy(k).wait_send())
+    for copy in stores:
+        copy.wait()
     each(n_ctx, lambda k: c_copy(k).wait_send())
     each(n_ctx, lambda k: p_copy(k).wait_send())
     if n_ctx > 2:
@@ -411,13 +445,12 @@
     width = inner // heads
     wcols = up(cols, 16)
     wide = rows % LANES == 0
-    wt = jnp.pad(w_in.T, ((0, wcols - cols), (0, 0)))
+    wt = w_in.T
     if not wide:
         tokens = jnp.swapaxes(tokens.reshape(t, n_dp, rows), 0, 1)
-    vec = jnp.pad(jnp.stack([a_log, dt_bias]), ((0, 6), (0, LANES - heads)))
-    dexp = jnp.repeat(d_skip, width)[None]
     cb = cols // n_ctx
-    cbp = up(cb, 8)
+    cbp = up(cb, 16)
+    part_rows = up(max(wcols, cols - cb + cbp), 8)
     vm = pltpu.VMEM
     n_a = n_dp // inner_group(n_dp)
     if not wide:
@@ -426,13 +459,22 @@
         wall = (n_ctx, wcols, n_dp * rows // n_ctx)
     else:
         wall = (wcols, n_dp * rows)
-    scratch = [
+    shapes = (
+        jax.ShapeDtypeStruct((t, inner), BF16),
+        jax.ShapeDtypeStruct((STATE, t), BF16),
+        jax.ShapeDtypeStruct((cols, t), BF16),
+        jax.ShapeDtypeStruct((cb, rows), F32),
+    )
+    n_b = inner_group(n_dp)
+    scratch = [vm(r.shape, r.dtype) for r in shapes] + [
+        vm((wcols, rows), BF16),
+        vm((8, LANES), F32),
         vm(tokens.shape, BF16),
         vm((t, inner), BF16),
         vm((t, inner), BF16),
         vm(wall, BF16),
-        vm((n_dp * t, rows), BF16),
-        vm((wcols, n_dp * t), BF16),
+        vm((n_a, n_b * t, rows), BF16),
+        vm((wcols, n_b * t), BF16),
         vm((2, STATE, inner), BF16),
         vm((n_ctx, STATE, inner), BF16),
         vm((inner // LANES, LANES // width * t, t), F32),
@@ -448,42 +490,39 @@
         vm((LANES, t), F32),
         vm((t, LANES), F32),
         vm((t, t), F32),
-        vm((wcols, rows), F32),
-        vm((n_ctx, cbp, rows), F32),
-        vm((n_ctx, cbp, rows), F32),
+        vm((n_a, part_rows, rows), F32),
+        vm((n_ctx, n_a, cbp, rows), BF16),
+        vm((n_ctx, n_a, cbp, rows), BF16),
+        vm((n_a, cbp, rows), BF16),
+        vm((n_a, cbp, rows), BF16),
         vm((8, LANES), F32),
         vm((n_ctx, 8, LANES), F32),
     ]
     dma = pltpu.SemaphoreType.DMA
-    scratch += [dma((n_a,))] * 2 + [dma((n_dp,))] * 4 + [dma((n_a,))] * 2 + [dma((n_dp,))] * 2
+    scratch += [dma((n_a,))] * 2 + [dma((n_dp,))] * 4 + [dma((n_a,))] * 2 + [dma((n_dp,))] * 2 + [dma((4,))]
     scratch += [dma((n_ctx,))] * 6 + [dma((n_a,))] * 2 + [dma((3,))]
     hbm = pl.BlockSpec(memory_space=pltpu.HBM)
     spec = pl.BlockSpec(memory_space=pltpu.VMEM)
     cfg = (n_dp, n_ctx, t, rows, heads, width, cols)
     results = pl.pallas_call(
         functools.partial(kernel, cfg),
-        out_shape=(
-            jax.ShapeDtypeStruct((t, inner), BF16),
-            jax.ShapeDtypeStruct((t, STATE), BF16),
-            jax.ShapeDtypeStruct((t, cols), BF16),
-            jax.ShapeDtypeStruct((rows, cb), F32),
-        ),
-        in_specs=[hbm] * 3 + [spec] * 4,
-        out_specs=(spec,) * 4,
+        out_shape=shapes,
+        in_specs=[hbm] * 3 + [spec] * 5,
+        out_specs=(hbm,) * 4,
         scratch_shapes=scratch,
         compiler_params=pltpu.CompilerParams(
-            collective_id=0, has_side_effects=True, vmem_limit_bytes=48 * 1024 * 1024),
+            collective_id=0, has_side_effects=True, vmem_limit_bytes=62 * 1024 * 1024),
         name="ssm_backward",
-    )(tokens, x, g, c, wt, vec, dexp)
+    )(tokens, x, g, c.T, wt, a_log[None], dt_bias[None], d_skip[None])
     gx, gc, gp, gw = pl.pallas_call(
         store,
         out_shape=tuple(jax.ShapeDtypeStruct(r.shape, r.dtype) for r in results),
-        in_specs=[spec] * 4,
+        in_specs=[pl.BlockSpec(memory_space=pl.ANY)] * 4,
         out_specs=(hbm,) * 4,
         scratch_shapes=[dma((4,))],
         name="store_results",
     )(*results)
-    return (gx[None], gc[None], gp[None], gw)
+    return (gx[None], gc.T[None], gp.T[None], gw.T)
 
 
 def solution(mesh):

time: 64.4 us -> 67.9 us (1.054)
  Pallas kernels: 52.5 us -> 67.1 us
  local copies, waits for them, and re-layouts: 10.1 us -> 0 us
  other arithmetic: 0.71 us -> 0 us
    pallas_call x1, Pallas kernels: 2.01 us -> 21.8 us  [per_device(): pl.pallas_call(store, out_shape=tuple((jax.ShapeDtypeStruct(r.shape, r.dt...]
    unnamed x26 -> x0, local copies, waits for them, and re-layouts: 9.91 us -> none
    pallas_call x1, Pallas kernels: 50.5 us -> 45.3 us  [per_device(): pl.pallas_call(functools.partial(kernel, cfg), out_shape=shapes, in_specs...]
    another operation x1 -> x0, other arithmetic: 0.71 us -> none  [per_device(): vec = jnp.pad(jnp.stack([a_log, dt_bias]), ((0, 6), (0, LANES - heads)))]
where the time goes in v3:
time: 67.9 us; the launch traced here: 67.7 us
  Pallas kernels  67.1 us (99%)
    pallas_call x1, Pallas kernels, per_device(): pl.pallas_call(functools.partial(kernel, cfg), out_shape=shapes, in_specs...  45.3 us
    pallas_call x1, Pallas kernels, per_device(): pl.pallas_call(store, out_shape=tuple((jax.ShapeDtypeStruct(r.shape, r.dt...  21.8 us

profile of v3, /device:TPU:0, one launch (start us, length us, event | category | flops | bytes accessed | tf_op | source)
XLA Modules:
  0.0 67.7 jit_solution(5734256952378972944)
XLA Ops:
  0.6 45.3 %ssm_backward.1 = (bf16[128,2176]{1,0:T(8,128)(2,1)}, bf16[64,128]{1,0:T(8,128)(2,1)}, bf16[132,128]{1,0:T(8,128)(2,1)}, f32[66,256]{1,0:T(8,128)}) custom-call(bf16[128,4096]{1,0:T(8,128)(2,1)} %bitcast.18, bf16[128,2176]{1,0:T(8,128)(2,1)} %bitcast.19, bf16[128,2176]{1,0:T(8,128)(2,1)} %bitcast.20, bf16[64,128]{1,0:T(8,128)(2,1)} %bitcast.22, ...), custom_call_target="tpu_custom_call" | custom-call | tf_op jit(solution)/shard_map/ssm_backward/pallas_call | solution.py:507
  45.9 21.8 %store_results.1 = (bf16[128,2176]{1,0:T(8,128)(2,1)}, bf16[64,128]{1,0:T(8,128)(2,1)}, bf16[132,128]{1,0:T(8,128)(2,1)}, f32[66,256]{1,0:T(8,128)}) custom-call(bf16[128,2176]{1,0:T(8,128)(2,1)} %get-tuple-element.12.refs_0_, bf16[64,128]{1,0:T(8,128)(2,1)} %get-tuple-element.13.refs_1_, bf16[132,128]{1,0:T(8,128)(2,1)} %get-tuple-element.14.refs_2_, ...), custom_call_target="tpu_custom_call" | custom-call | tf_op jit(solution)/shard_map/store_results/pallas_call | solution.py:517

commit v4 on v3

--- a/solution.py
+++ b/solution.py
@@ -428,9 +428,13 @@
 
 
 def store(*refs):
-    sems = refs[-1]
-    copies = [pltpu.make_async_copy(refs[i], refs[4 + i], sems.at[i]) for i in range(4)]
-    for copy in copies:
+    held, sems = refs[8:12], refs[-1]
+    loads = [pltpu.make_async_copy(refs[i], held[i], sems.at[0, i]) for i in range(4)]
+    copies = [pltpu.make_async_copy(held[i], refs[4 + i], sems.at[1, i]) for i in range(4)]
+    for load in loads:
+        load.start()
+    for load, copy in zip(loads, copies):
+        load.wait()
         copy.start()
     for copy in copies:
         copy.wait()
@@ -519,7 +523,7 @@
         out_shape=tuple(jax.ShapeDtypeStruct(r.shape, r.dtype) for r in results),
         in_specs=[pl.BlockSpec(memory_space=pl.ANY)] * 4,
         out_specs=(hbm,) * 4,
-        scratch_shapes=[dma((4,))],
+        scratch_shapes=[vm(r.shape, r.dtype) for r in shapes] + [dma((2, 4))],
         name="store_results",
     )(*results)
     return (gx[None], gc.T[None], gp.T[None], gw.T)

time: 67.9 us -> 48.1 us (0.71)
  Pallas kernels: 67.1 us -> 47.3 us
    pallas_call x1, Pallas kernels: 21.8 us -> 1.96 us  [per_device(): pl.pallas_call(store, out_shape=tuple((jax.ShapeDtypeStruct(r.shape, r.dt...]
where the time goes in v4:
time: 48.1 us; the launch traced here: 47.9 us
  Pallas kernels  47.3 us (98%)
  between operations  0.64 us (1%)
    pallas_call x1, Pallas kernels, per_device(): pl.pallas_call(functools.partial(kernel, cfg), out_shape=shapes, in_specs...  45.3 us
    pallas_call x1, Pallas kernels, per_device(): pl.pallas_call(store, out_shape=tuple((jax.ShapeDtypeStruct(r.shape, r.dt...  1.96 us

profile of v4, /device:TPU:0, one launch (start us, length us, event | category | flops | bytes accessed | tf_op | source)
XLA Modules:
  0.0 47.9 jit_solution(11650204890052052686)
XLA Ops:
  0.6 45.3 %ssm_backward.1 = (bf16[128,2176]{1,0:T(8,128)(2,1)}, bf16[64,128]{1,0:T(8,128)(2,1)}, bf16[132,128]{1,0:T(8,128)(2,1)}, f32[66,256]{1,0:T(8,128)}) custom-call(bf16[128,4096]{1,0:T(8,128)(2,1)} %bitcast.18, bf16[128,2176]{1,0:T(8,128)(2,1)} %bitcast.19, bf16[128,2176]{1,0:T(8,128)(2,1)} %bitcast.20, bf16[64,128]{1,0:T(8,128)(2,1)} %bitcast.22, ...), custom_call_target="tpu_custom_call" | custom-call | tf_op jit(solution)/shard_map/ssm_backward/pallas_call | solution.py:511
  45.9 2.0 %store_results.1 = (bf16[128,2176]{1,0:T(8,128)(2,1)}, bf16[64,128]{1,0:T(8,128)(2,1)}, bf16[132,128]{1,0:T(8,128)(2,1)}, f32[66,256]{1,0:T(8,128)}) custom-call(bf16[128,2176]{1,0:T(8,128)(2,1)} %get-tuple-element.12.refs_0_, bf16[64,128]{1,0:T(8,128)(2,1)} %get-tuple-element.13.refs_1_, bf16[132,128]{1,0:T(8,128)(2,1)} %get-tuple-element.14.refs_2_, ...), custom_call_target="tpu_custom_call" | custom-call | tf_op jit(solution)/shard_map/store_results/pallas_call | solution.py:521
